TPU v7x, 32 devices: a whole 2x2x4 slice. The times are simulated.
32 devices in a mesh: grp: 4 (over y, x), col: 8 (over z, core).
Axes of the slice: x: 2, y: 2, z: 4, core: 2. Of those that a mesh axis runs over, the one named last changes fastest.
Arguments:
- start_block: float32 [16, 8192], P(None, ('grp', 'col')), may hold values from -6 to 6
- tile_values: float32 [4, 8, 32, 256, 256], P('grp', 'col'), may hold values from 0 to 1, as said below
- tile_row: int32 [4, 8, 32], P('grp', 'col'), may hold values from 0 to 31, as said below
- tile_col: int32 [4, 8, 32], P('grp', 'col'), may hold values from 0 to 31, as said below
- tile_count: int32 [4, 8], P('grp', 'col'), may hold values from 8 to 32, as said below
Outputs:
- basis: float32 [5, 16, 8192], P(None, None, ('grp', 'col'))
- projections: float32 [4, 4, 16, 16], replicated
- factors: float32 [5, 16, 16], replicated
Inputs may be any that keep to these rules, and one draw needn't show every extreme that they name: `tile_row`: A tile of the device at grp index g lies in tile rows g * 8 * 1 to (g + 1) * 8 - 1. `tile_col`: A tile column t of the device at col index c has (t) % 8 == c. Coordinate pairs may repeat; repeated tiles add. The live tiles of a device are its first tile_count slots; some device has all 32 slots live. `tile_values`: entries are nonnegative.
All inputs are finite; a program needn't handle non-finite values.
Results may differ from a plain program's by a relative error of at most 0.0003.
Values sent between devices are 32-bit elements; how exact they have to be, the bound alone decides.
A program may use at most 64 MiB of HBM per device.

v0:
```python
import jax
import jax.numpy as jnp
from jax import lax
from jax.sharding import PartitionSpec as P

ITERS = 4
highest = lax.Precision.HIGHEST


def select_rows(selector, panel, tile_size):
    block_rows = panel.shape[0]
    shaped = panel.reshape(block_rows, -1, tile_size)
    return jnp.einsum("sr,qrt->qst", selector, shaped, precision=highest)


def spread_rows(selector, pieces):
    block_rows = pieces.shape[0]
    placed = jnp.einsum("sr,qst->qrt", selector, pieces, precision=highest)
    return placed.reshape(block_rows, -1)


def orthonormal(block_rows, gram_now):
    factor = jnp.linalg.cholesky(gram_now)
    solved = jax.scipy.linalg.solve_triangular(factor, block_rows, lower=True)
    return (solved, factor)


def body(start_block, tile_values, tile_row, tile_col, tile_count):
    grp_size = lax.axis_size("grp")
    col_size = lax.axis_size("col")
    grp_index = lax.axis_index("grp")
    tile_data = tile_values[0, 0]
    tile_size = tile_data.shape[-1]
    slot_count = tile_data.shape[0]
    shard_len = start_block.shape[1]
    row_tiles = shard_len // tile_size
    node_total = shard_len * grp_size * col_size
    live_slot = (jnp.arange(slot_count, dtype=jnp.int32) < tile_count[0, 0]).astype(jnp.float32)
    local_row = tile_row[0, 0] - grp_index * (col_size * row_tiles)
    global_col = tile_col[0, 0]
    local_col = global_col // (row_tiles * col_size) * row_tiles + global_col % row_tiles
    row_places = jnp.arange(col_size * row_tiles, dtype=jnp.int32)
    col_places = jnp.arange(grp_size * row_tiles, dtype=jnp.int32)
    row_select = (local_row[:, None] == row_places[None, :]).astype(jnp.float32) * live_slot[
        :, None
    ]
    col_select = (local_col[:, None] == col_places[None, :]).astype(jnp.float32) * live_slot[
        :, None
    ]

    def combine(part_rows, part_cols):
        mine_rows = lax.psum_scatter(part_rows, "col", scatter_dimension=1, tiled=True)
        mine_cols = lax.psum_scatter(part_cols, "grp", scatter_dimension=1, tiled=True)
        return mine_rows + mine_cols

    row_totals = jnp.sum(tile_data, axis=2)[None]
    col_totals = jnp.sum(tile_data, axis=1)[None]
    degree = combine(spread_rows(row_select, row_totals), spread_rows(col_select, col_totals))
    start_gram = (
        lax.psum(jnp.dot(start_block, start_block.T, precision=highest), ("grp", "col"))
        / node_total
    )
    first_block, factor = orthonormal(start_block, start_gram)
    block_width = start_block.shape[0]
    basis_list = [first_block]
    factor_list = [factor]
    projections = jnp.zeros((ITERS, ITERS, block_width, block_width), jnp.float32)
    for step_index in range(ITERS):
        laplace_vector = basis_list[-1]
        row_panel = lax.all_gather(laplace_vector, "col", axis=1, tiled=True)
        col_panel = lax.all_gather(laplace_vector, "grp", axis=1, tiled=True)
        at_cols = select_rows(col_select, col_panel, tile_size)
        at_rows = select_rows(row_select, row_panel, tile_size)
        into_rows = jnp.einsum("sij,qsj->qsi", tile_data, at_cols, precision=highest)
        into_cols = jnp.einsum("sij,qsi->qsj", tile_data, at_rows, precision=highest)
        product = combine(spread_rows(row_select, into_rows), spread_rows(col_select, into_cols))
        applied = degree * laplace_vector - product
        stacked = jnp.stack(basis_list)
        coeff_part = jnp.einsum("an,jbn->jab", applied, stacked, precision=highest)
        coeffs = lax.psum(coeff_part, ("grp", "col")) / node_total
        applied = applied - jnp.einsum("jab,jbn->an", coeffs, stacked, precision=highest)
        gram_now = (
            lax.psum(jnp.dot(applied, applied.T, precision=highest), ("grp", "col")) / node_total
        )
        next_block, factor = orthonormal(applied, gram_now)
        basis_list.append(next_block)
        factor_list.append(factor)
        projections = projections.at[step_index, : step_index + 1].set(coeffs)
    return (jnp.stack(basis_list), projections, jnp.stack(factor_list))


def solution(mesh):
    in_specs = (
        P(None, ("grp", "col")),
        P("grp", "col", None, None, None),
        P("grp", "col", None),
        P("grp", "col", None),
        P("grp", "col"),
    )
    out_specs = (P(None, None, ("grp", "col")), P(), P())
    return jax.shard_map(body, mesh=mesh, in_specs=in_specs, out_specs=out_specs, check_vma=False)
```

profile of v0, /device:TPU:0, one launch (start us, length us, event | category | flops | bytes accessed | tf_op | source)
XLA Modules:
  0.0 785.5 jit_solution(12459310264060773894)
XLA Ops:
  16.3 42.0 %psum.63 = f32[16,16]{0,1:T(8,128)S(1)} all-reduce(f32[16,16]{0,1:T(8,128)S(1)} %fusion.181), channel_id=1, replica_groups=mesh['grp'=4,'col'=8] {'grp','col'}, use_global_device_ids=true, to_apply=%region_0.1 | all-reduce | flops 256 | bytes 2048 | tf_op jit(solution)/shard_map/psum | solution.py:60
  62.6 14.2 %all_gather.25 = f32[16,2048]{1,0:T(8,128)S(1)} all-gather(f32[16,256]{1,0:T(8,128)S(1)} %get-tuple-element.65), channel_id=1, replica_groups=mesh['grp'=4,'col'=8] {'col'}, dimensions={1}, use_global_device_ids=true | all-gather | bytes 147456 | tf_op jit(solution)/shard_map/all_gather | solution.py:70
  95.3 9.5 %fusion.16 = f32[16,32,256]{2,0,1:T(8,128)S(1)} fusion(f32[1,1,32,256,256]{4,3,2,1,0:T(8,128)} %param.17, f32[16,32,256]{2,1,0:T(8,128)S(1)} %convolution_bitcast_fusion.7), kind=kOutput, calls=%fused_computation.16 | convolution fusion | flops 402653184 | bytes 9437184 | tf_op jit(solution)/shard_map/sij,qsj->qsi/dot_general | solution.py:74
  109.4 33.3 %reduce-scatter.15.cloned.1.call-done = f32[16,256]{1,0:T(8,128)} async-done(((f32[16,2048]{1,0:T(8,128)}), f32[16,256]{1,0:T(8,128)}) %reduce-scatter.15.cloned.1.call-update) | async-done | bytes 16400 | tf_op jit(solution)/shard_map/reduce_scatter | solution.py:52
  143.5 37.9 %psum.64 = f32[1,16,16]{1,2,0:T(8,128)S(1)} all-reduce(f32[1,16,16]{1,2,0:T(8,128)S(1)} %convolution_bitcast_fusion.15), channel_id=1, replica_groups=mesh['grp'=4,'col'=8] {'grp','col'}, use_global_device_ids=true, to_apply=%region_9.12 | all-reduce | flops 256 | bytes 2048 | tf_op jit(solution)/shard_map/psum | solution.py:80
  182.5 41.3 %psum.65 = f32[16,16]{0,1:T(8,128)S(1)} all-reduce(f32[16,16]{0,1:T(8,128)S(1)} %fusion.182), channel_id=1, replica_groups=mesh['grp'=4,'col'=8] {'grp','col'}, use_global_device_ids=true, to_apply=%region_10.13 | all-reduce | flops 256 | bytes 2048 | tf_op jit(solution)/shard_map/psum | solution.py:83
  237.1 13.9 %all_gather.27 = f32[16,2048]{1,0:T(8,128)S(1)} all-gather(f32[16,256]{1,0:T(8,128)S(1)} %get-tuple-element.67), channel_id=1, replica_groups=mesh['grp'=4,'col'=8] {'col'}, dimensions={1}, use_global_device_ids=true | all-gather | bytes 147456 | tf_op jit(solution)/shard_map/all_gather | solution.py:70
  251.7 9.5 %fusion.22 = f32[16,32,256]{2,0,1:T(8,128)S(1)} fusion(f32[1,1,32,256,256]{4,3,2,1,0:T(8,128)} %param.17, f32[16,32,256]{2,1,0:T(8,128)S(1)} %convolution_bitcast_fusion.6), kind=kOutput, calls=%fused_computation.18 | convolution fusion | flops 402653184 | bytes 9437184 | tf_op jit(solution)/shard_map/sij,qsj->qsi/dot_general | solution.py:74
  272.0 20.4 %reduce-scatter.21.cloned.1.call-done = f32[16,256]{1,0:T(8,128)} async-done(((f32[16,1024]{1,0:T(8,128)}), f32[16,256]{1,0:T(8,128)}) %reduce-scatter.21.cloned.1.call-update) | async-done | bytes 16400 | tf_op jit(solution)/shard_map/reduce_scatter | solution.py:53
  292.4 33.3 %reduce-scatter.19.cloned.1.call-done = f32[16,256]{1,0:T(8,128)} async-done(((f32[16,2048]{1,0:T(8,128)}), f32[16,256]{1,0:T(8,128)}) %reduce-scatter.19.cloned.1.call-update) | async-done | bytes 16400 | tf_op jit(solution)/shard_map/reduce_scatter | solution.py:52
  326.6 37.8 %psum.66 = f32[2,16,16]{1,2,0:T(8,128)S(1)} all-reduce(f32[2,16,16]{1,2,0:T(8,128)S(1)} %convolution_bitcast_fusion.14), channel_id=1, replica_groups=mesh['grp'=4,'col'=8] {'grp','col'}, use_global_device_ids=true, to_apply=%region_13.16 | all-reduce | flops 512 | bytes 4096 | tf_op jit(solution)/shard_map/psum | solution.py:80
  364.8 41.6 %psum.67 = f32[16,16]{0,1:T(8,128)S(1)} all-reduce(f32[16,16]{0,1:T(8,128)S(1)} %fusion.183), channel_id=1, replica_groups=mesh['grp'=4,'col'=8] {'grp','col'}, use_global_device_ids=true, to_apply=%region_14.17 | all-reduce | flops 256 | bytes 2048 | tf_op jit(solution)/shard_map/psum | solution.py:83
  419.7 13.9 %all_gather.29 = f32[16,2048]{1,0:T(8,128)S(1)} all-gather(f32[16,256]{1,0:T(8,128)S(1)} %get-tuple-element.69), channel_id=1, replica_groups=mesh['grp'=4,'col'=8] {'col'}, dimensions={1}, use_global_device_ids=true | all-gather | bytes 147456 | tf_op jit(solution)/shard_map/all_gather | solution.py:70
  434.3 9.5 %fusion.28 = f32[16,32,256]{2,0,1:T(8,128)S(1)} fusion(f32[1,1,32,256,256]{4,3,2,1,0:T(8,128)} %param.17, f32[16,32,256]{2,1,0:T(8,128)S(1)} %convolution_bitcast_fusion.5), kind=kOutput, calls=%fused_computation.20 | convolution fusion | flops 402653184 | bytes 9437184 | tf_op jit(solution)/shard_map/sij,qsj->qsi/dot_general | solution.py:74
  454.7 20.3 %reduce-scatter.25.cloned.1.call-done = f32[16,256]{1,0:T(8,128)} async-done(((f32[16,1024]{1,0:T(8,128)}), f32[16,256]{1,0:T(8,128)}) %reduce-scatter.25.cloned.1.call-update) | async-done | bytes 16400 | tf_op jit(solution)/shard_map/reduce_scatter | solution.py:53
  474.9 33.5 %reduce-scatter.23.cloned.1.call-done = f32[16,256]{1,0:T(8,128)} async-done(((f32[16,2048]{1,0:T(8,128)}), f32[16,256]{1,0:T(8,128)}) %reduce-scatter.23.cloned.1.call-update) | async-done | bytes 16400 | tf_op jit(solution)/shard_map/reduce_scatter | solution.py:52
  509.4 37.9 %psum.68 = f32[3,16,16]{1,2,0:T(8,128)S(1)} all-reduce(f32[3,16,16]{1,2,0:T(8,128)S(1)} %convolution_bitcast_fusion.9), channel_id=1, replica_groups=mesh['grp'=4,'col'=8] {'grp','col'}, use_global_device_ids=true, to_apply=%region_17.20 | all-reduce | flops 768 | bytes 6144 | tf_op jit(solution)/shard_map/psum | solution.py:80
  547.6 41.4 %psum.69 = f32[16,16]{0,1:T(8,128)S(1)} all-reduce(f32[16,16]{0,1:T(8,128)S(1)} %fusion.184), channel_id=1, replica_groups=mesh['grp'=4,'col'=8] {'grp','col'}, use_global_device_ids=true, to_apply=%region_18.21 | all-reduce | flops 256 | bytes 2048 | tf_op jit(solution)/shard_map/psum | solution.py:83
  602.4 14.2 %all_gather.31 = f32[16,2048]{1,0:T(8,128)S(1)} all-gather(f32[16,256]{1,0:T(8,128)S(1)} %get-tuple-element.71), channel_id=1, replica_groups=mesh['grp'=4,'col'=8] {'col'}, dimensions={1}, use_global_device_ids=true | all-gather | bytes 147456 | tf_op jit(solution)/shard_map/all_gather | solution.py:70
  617.2 9.5 %fusion.34 = f32[16,32,256]{2,0,1:T(8,128)S(1)} fusion(f32[1,1,32,256,256]{4,3,2,1,0:T(8,128)} %param.17, f32[16,32,256]{2,1,0:T(8,128)S(1)} %convolution_bitcast_fusion.4), kind=kOutput, calls=%fused_computation.22 | convolution fusion | flops 402653184 | bytes 9437184 | tf_op jit(solution)/shard_map/sij,qsj->qsi/dot_general | solution.py:74
  637.5 20.4 %reduce-scatter.29.cloned.1.call-done = f32[16,256]{1,0:T(8,128)} async-done(((f32[16,1024]{1,0:T(8,128)}), f32[16,256]{1,0:T(8,128)}) %reduce-scatter.29.cloned.1.call-update) | async-done | bytes 16400 | tf_op jit(solution)/shard_map/reduce_scatter | solution.py:53
  657.8 33.3 %reduce-scatter.27.cloned.1.call-done = f32[16,256]{1,0:T(8,128)} async-done(((f32[16,2048]{1,0:T(8,128)}), f32[16,256]{1,0:T(8,128)}) %reduce-scatter.27.cloned.1.call-update) | async-done | bytes 16400 | tf_op jit(solution)/shard_map/reduce_scatter | solution.py:52
  692.0 37.9 %psum.70 = f32[4,16,16]{1,2,0:T(8,128)S(1)} all-reduce(f32[4,16,16]{1,2,0:T(8,128)S(1)} %convolution_bitcast_fusion.8), channel_id=1, replica_groups=mesh['grp'=4,'col'=8] {'grp','col'}, use_global_device_ids=true, to_apply=%region_21.24 | all-reduce | flops 1024 | bytes 8192 | tf_op jit(solution)/shard_map/psum | solution.py:80
  730.3 41.4 %psum.71 = f32[16,16]{0,1:T(8,128)S(1)} all-reduce(f32[16,16]{0,1:T(8,128)S(1)} %fusion.185), channel_id=1, replica_groups=mesh['grp'=4,'col'=8] {'grp','col'}, use_global_device_ids=true, to_apply=%region_22.25 | all-reduce | flops 256 | bytes 2048 | tf_op jit(solution)/shard_map/psum | solution.py:83
  (158 shorter events, 122.3 us)
Async XLA Ops:
  7.2 9.0 %copy-start = (f32[16,256]{1,0:T(8,128)S(1)}, f32[16,256]{1,0:T(8,128)}, u32[]{:S(2)}) copy-start(f32[16,256]{1,0:T(8,128)} %param.16) | copy-start | bytes 49156
  7.2 7.3 copy-start.3
  7.2 100.2 %reduce-scatter.33.cloned.1.call-start = ((), (), s32[]{:S(2)}) async-start(), calls=%async_computation.19 | async-start | bytes 655360
  14.4 94.0 %reduce-scatter.31.cloned.1.call-start = ((), (), s32[]{:S(2)}) async-start(), calls=%async_computation.18 | async-start | bytes 1179648
  16.1 93.3 %reduce-scatter.17.cloned.1.call-start = ((), (), s32[]{:S(2)}) async-start(), calls=%async_computation.11 | async-start | bytes 81920 | tf_op jit(solution)/shard_map/reduce_scatter | solution.py:53
  85.4 57.2 %reduce-scatter.15.cloned.1.call-start = ((), (), s32[]{:S(2)}) async-start(), calls=%async_computation.10 | async-start | bytes 147456 | tf_op jit(solution)/shard_map/reduce_scatter | solution.py:52
  106.2 186.2 %reduce-scatter.21.cloned.1.call-start = ((), (), s32[]{:S(2)}) async-start(), calls=%async_computation.13 | async-start | bytes 81920 | tf_op jit(solution)/shard_map/reduce_scatter | solution.py:53
  269.9 55.9 %reduce-scatter.19.cloned.1.call-start = ((), (), s32[]{:S(2)}) async-start(), calls=%async_computation.12 | async-start | bytes 147456 | tf_op jit(solution)/shard_map/reduce_scatter | solution.py:52
  271.3 203.6 %reduce-scatter.25.cloned.1.call-start = ((), (), s32[]{:S(2)}) async-start(), calls=%async_computation.15 | async-start | bytes 81920 | tf_op jit(solution)/shard_map/reduce_scatter | solution.py:53
  452.5 55.9 %reduce-scatter.23.cloned.1.call-start = ((), (), s32[]{:S(2)}) async-start(), calls=%async_computation.14 | async-start | bytes 147456 | tf_op jit(solution)/shard_map/reduce_scatter | solution.py:52
  453.9 203.9 %reduce-scatter.29.cloned.1.call-start = ((), (), s32[]{:S(2)}) async-start(), calls=%async_computation.17 | async-start | bytes 81920 | tf_op jit(solution)/shard_map/reduce_scatter | solution.py:53
  635.3 55.8 %reduce-scatter.27.cloned.1.call-start = ((), (), s32[]{:S(2)}) async-start(), calls=%async_computation.16 | async-start | bytes 147456 | tf_op jit(solution)/shard_map/reduce_scatter | solution.py:52
  777.2 0.6 copy-start.2
  777.8 0.6 copy-start.1
Sparse Core Ops, SparseCore 0:
  14.5 27.8 reduce-scatter.32
  44.6 32.9 reduce-scatter.30
  85.6 23.7 reduce-scatter.16
  112.0 30.5 reduce-scatter.14
  270.0 22.3 reduce-scatter.20
  295.1 30.5 reduce-scatter.18
  452.6 22.2 reduce-scatter.24
  477.7 30.6 reduce-scatter.22
  635.5 22.3 reduce-scatter.28
  660.5 30.5 reduce-scatter.26
where the time goes:
time: 797 us; the launch traced here: 786 us
  blocking collectives  452 us (57%)
  waiting for transfers between devices  195 us (24%)
  matrix products  79.7 us (10%)
  other arithmetic  30.8 us (4%)
  between operations  15.5 us (2%)
  local copies, waits for them, and re-layouts  12.4 us (2%)
    psum x4, blocking collectives, body(): lax.psum(jnp.dot(applied, applied.T, precision=highest), ('grp', 'col'))  166 us
    psum x4, blocking collectives, body(): coeffs = lax.psum(coeff_part, ('grp', 'col')) / node_total  152 us
    reduce_scatter x4, waiting for transfers between devices, combine(): lax.psum_scatter(part_rows, 'col', scatter_dimension=1, tiled=True)  133 us
    reduce_scatter x4, waiting for transfers between devices, combine(): lax.psum_scatter(part_cols, 'grp', scatter_dimension=1, tiled=True)  61 us
    all_gather x4, blocking collectives, body(): row_panel = lax.all_gather(laplace_vector, 'col', axis=1, tiled=True)  56.3 us
    psum x1, blocking collectives, body(): lax.psum(jnp.dot(start_block, start_block.T, precision=highest), ('grp',...  42 us
    dot_general x4, matrix products, body(): jnp.einsum('sij,qsj->qsi', tile_data, at_cols, precision=highest)  37.9 us
    all_gather x4, blocking collectives, body(): col_panel = lax.all_gather(laplace_vector, 'grp', axis=1, tiled=True)  36.2 us
  transfers between devices with their start and end apart: 10, of which 7 were waited for; matrix products, arithmetic and copies ran while one was open for 4% of the time, Pallas kernels for 0%

commit v1 on v0

--- a/solution.py
+++ b/solution.py
@@ -1,10 +1,20 @@
+import functools
 import jax
 import jax.numpy as jnp
 from jax import lax
 from jax.sharding import PartitionSpec as P
+from jax.lax import psum
 
 ITERS = 4
 highest = lax.Precision.HIGHEST
+
+
+def proceed_the_masks(slab_in, axis_tag, device_axis):
+    val = psum(psum(slab_in, axis_name=axis_tag), device_axis)
+    return val
+
+
+feed_axis_part = functools.partial(proceed_the_masks, axis_tag="grp", device_axis="col")
 
 
 def select_rows(selector, panel, tile_size):
@@ -56,10 +66,7 @@
     row_totals = jnp.sum(tile_data, axis=2)[None]
     col_totals = jnp.sum(tile_data, axis=1)[None]
     degree = combine(spread_rows(row_select, row_totals), spread_rows(col_select, col_totals))
-    start_gram = (
-        lax.psum(jnp.dot(start_block, start_block.T, precision=highest), ("grp", "col"))
-        / node_total
-    )
+    start_gram = feed_axis_part(jnp.dot(start_block, start_block.T, precision=highest)) / node_total
     first_block, factor = orthonormal(start_block, start_gram)
     block_width = start_block.shape[0]
     basis_list = [first_block]

time: 797 us -> 790 us (level)
  blocking collectives: 452 us -> 435 us
  waiting for transfers between devices: 195 us -> 206 us
    psum x1 -> x2, blocking collectives: 42 us -> 26.5 us  [proceed_the_masks(): val = psum(psum(slab_in, axis_name=axis_tag), device_axis)]
    reduce_scatter x4, waiting for transfers between devices: 61 us -> 72.6 us  [combine(): lax.psum_scatter(part_cols, 'grp', scatter_dimension=1, tiled=True)]
  transfers between devices with their start and end apart: 10 -> 10, of which waited for: 7 -> 8; matrix products, arithmetic and copies ran while one was open for 4% -> 4% of each run, Pallas kernels for 0% -> 0%
where the time goes in v1:
time: 790 us; the launch traced here: 780 us
  blocking collectives  435 us (55%)
  waiting for transfers between devices  206 us (26%)
  matrix products  79.8 us (10%)
  other arithmetic  30.8 us (4%)
  between operations  15.6 us (2%)
  local copies, waits for them, and re-layouts  12.4 us (2%)
    psum x4, blocking collectives, body(): lax.psum(jnp.dot(applied, applied.T, precision=highest), ('grp', 'col'))  166 us
    psum x4, blocking collectives, body(): coeffs = lax.psum(coeff_part, ('grp', 'col')) / node_total  152 us
    reduce_scatter x4, waiting for transfers between devices, combine(): lax.psum_scatter(part_rows, 'col', scatter_dimension=1, tiled=True)  133 us
    reduce_scatter x4, waiting for transfers between devices, combine(): lax.psum_scatter(part_cols, 'grp', scatter_dimension=1, tiled=True)  72.6 us
    all_gather x4, blocking collectives, body(): row_panel = lax.all_gather(laplace_vector, 'col', axis=1, tiled=True)  56.2 us
    dot_general x4, matrix products, body(): jnp.einsum('sij,qsj->qsi', tile_data, at_cols, precision=highest)  37.9 us
    all_gather x4, blocking collectives, body(): col_panel = lax.all_gather(laplace_vector, 'grp', axis=1, tiled=True)  34.3 us
    dot_general x4, matrix products, body(): jnp.einsum('sij,qsi->qsj', tile_data, at_rows, precision=highest)  26.6 us
  transfers between devices with their start and end apart: 10, of which 8 were waited for; matrix products, arithmetic and copies ran while one was open for 4% of the time, Pallas kernels for 0%

profile of v1, /device:TPU:0, one launch (start us, length us, event | category | flops | bytes accessed | tf_op | source)
XLA Modules:
  0.0 779.7 jit_solution(1161211626038431396)
XLA Ops:
  16.3 11.6 %psum.70 = f32[16,16]{0,1:T(8,128)S(1)} all-reduce(f32[16,16]{0,1:T(8,128)S(1)} %fusion.181), channel_id=1, replica_groups=mesh['grp'=4,'col'=8] {'grp'}, use_global_device_ids=true, to_apply=%region_0.1 | all-reduce | flops 256 | bytes 2048 | tf_op jit(solution)/shard_map/psum | solution.py:13
  27.9 14.9 %psum.71 = f32[16,16]{0,1:T(8,128)S(1)} all-reduce(f32[16,16]{0,1:T(8,128)S(1)} %psum.70), channel_id=1, replica_groups=mesh['grp'=4,'col'=8] {'col'}, use_global_device_ids=true, to_apply=%region_1.2 | all-reduce | flops 256 | bytes 2048 | tf_op jit(solution)/shard_map/psum | solution.py:13
  47.1 14.1 %all_gather.25 = f32[16,2048]{1,0:T(8,128)S(1)} all-gather(f32[16,256]{1,0:T(8,128)S(1)} %get-tuple-element.65), channel_id=1, replica_groups=mesh['grp'=4,'col'=8] {'col'}, dimensions={1}, use_global_device_ids=true | all-gather | bytes 147456 | tf_op jit(solution)/shard_map/all_gather | solution.py:77
  91.5 11.6 %reduce-scatter.17.cloned.1.call-done = f32[16,256]{1,0:T(8,128)} async-done(((f32[16,1024]{1,0:T(8,128)}), f32[16,256]{1,0:T(8,128)}) %reduce-scatter.17.cloned.1.call-update) | async-done | bytes 16400 | tf_op jit(solution)/shard_map/reduce_scatter | solution.py:63
  103.1 33.3 %reduce-scatter.15.cloned.1.call-done = f32[16,256]{1,0:T(8,128)} async-done(((f32[16,2048]{1,0:T(8,128)}), f32[16,256]{1,0:T(8,128)}) %reduce-scatter.15.cloned.1.call-update) | async-done | bytes 16400 | tf_op jit(solution)/shard_map/reduce_scatter | solution.py:62
  137.2 38.3 %psum.72 = f32[1,16,16]{1,2,0:T(8,128)S(1)} all-reduce(f32[1,16,16]{1,2,0:T(8,128)S(1)} %convolution_bitcast_fusion.15), channel_id=1, replica_groups=mesh['grp'=4,'col'=8] {'grp','col'}, use_global_device_ids=true, to_apply=%region_10.13 | all-reduce | flops 256 | bytes 2048 | tf_op jit(solution)/shard_map/psum | solution.py:87
  176.6 41.4 %psum.73 = f32[16,16]{0,1:T(8,128)S(1)} all-reduce(f32[16,16]{0,1:T(8,128)S(1)} %fusion.182), channel_id=1, replica_groups=mesh['grp'=4,'col'=8] {'grp','col'}, use_global_device_ids=true, to_apply=%region_11.14 | all-reduce | flops 256 | bytes 2048 | tf_op jit(solution)/shard_map/psum | solution.py:90
  231.3 13.9 %all_gather.27 = f32[16,2048]{1,0:T(8,128)S(1)} all-gather(f32[16,256]{1,0:T(8,128)S(1)} %get-tuple-element.67), channel_id=1, replica_groups=mesh['grp'=4,'col'=8] {'col'}, dimensions={1}, use_global_device_ids=true | all-gather | bytes 147456 | tf_op jit(solution)/shard_map/all_gather | solution.py:77
  245.9 9.5 %fusion.22 = f32[16,32,256]{2,0,1:T(8,128)S(1)} fusion(f32[1,1,32,256,256]{4,3,2,1,0:T(8,128)} %param.17, f32[16,32,256]{2,1,0:T(8,128)S(1)} %convolution_bitcast_fusion.6), kind=kOutput, calls=%fused_computation.18 | convolution fusion | flops 402653184 | bytes 9437184 | tf_op jit(solution)/shard_map/sij,qsj->qsi/dot_general | solution.py:81
  266.3 20.3 %reduce-scatter.21.cloned.1.call-done = f32[16,256]{1,0:T(8,128)} async-done(((f32[16,1024]{1,0:T(8,128)}), f32[16,256]{1,0:T(8,128)}) %reduce-scatter.21.cloned.1.call-update) | async-done | bytes 16400 | tf_op jit(solution)/shard_map/reduce_scatter | solution.py:63
  286.6 33.3 %reduce-scatter.19.cloned.1.call-done = f32[16,256]{1,0:T(8,128)} async-done(((f32[16,2048]{1,0:T(8,128)}), f32[16,256]{1,0:T(8,128)}) %reduce-scatter.19.cloned.1.call-update) | async-done | bytes 16400 | tf_op jit(solution)/shard_map/reduce_scatter | solution.py:62
  320.8 37.8 %psum.74 = f32[2,16,16]{1,2,0:T(8,128)S(1)} all-reduce(f32[2,16,16]{1,2,0:T(8,128)S(1)} %convolution_bitcast_fusion.14), channel_id=1, replica_groups=mesh['grp'=4,'col'=8] {'grp','col'}, use_global_device_ids=true, to_apply=%region_14.17 | all-reduce | flops 512 | bytes 4096 | tf_op jit(solution)/shard_map/psum | solution.py:87
  358.9 41.6 %psum.75 = f32[16,16]{0,1:T(8,128)S(1)} all-reduce(f32[16,16]{0,1:T(8,128)S(1)} %fusion.183), channel_id=1, replica_groups=mesh['grp'=4,'col'=8] {'grp','col'}, use_global_device_ids=true, to_apply=%region_15.18 | all-reduce | flops 256 | bytes 2048 | tf_op jit(solution)/shard_map/psum | solution.py:90
  413.8 13.9 %all_gather.29 = f32[16,2048]{1,0:T(8,128)S(1)} all-gather(f32[16,256]{1,0:T(8,128)S(1)} %get-tuple-element.69), channel_id=1, replica_groups=mesh['grp'=4,'col'=8] {'col'}, dimensions={1}, use_global_device_ids=true | all-gather | bytes 147456 | tf_op jit(solution)/shard_map/all_gather | solution.py:77
  428.5 9.5 %fusion.28 = f32[16,32,256]{2,0,1:T(8,128)S(1)} fusion(f32[1,1,32,256,256]{4,3,2,1,0:T(8,128)} %param.17, f32[16,32,256]{2,1,0:T(8,128)S(1)} %convolution_bitcast_fusion.5), kind=kOutput, calls=%fused_computation.20 | convolution fusion | flops 402653184 | bytes 9437184 | tf_op jit(solution)/shard_map/sij,qsj->qsi/dot_general | solution.py:81
  448.8 20.3 %reduce-scatter.25.cloned.1.call-done = f32[16,256]{1,0:T(8,128)} async-done(((f32[16,1024]{1,0:T(8,128)}), f32[16,256]{1,0:T(8,128)}) %reduce-scatter.25.cloned.1.call-update) | async-done | bytes 16400 | tf_op jit(solution)/shard_map/reduce_scatter | solution.py:63
  469.1 33.4 %reduce-scatter.23.cloned.1.call-done = f32[16,256]{1,0:T(8,128)} async-done(((f32[16,2048]{1,0:T(8,128)}), f32[16,256]{1,0:T(8,128)}) %reduce-scatter.23.cloned.1.call-update) | async-done | bytes 16400 | tf_op jit(solution)/shard_map/reduce_scatter | solution.py:62
  503.4 38.0 %psum.76 = f32[3,16,16]{1,2,0:T(8,128)S(1)} all-reduce(f32[3,16,16]{1,2,0:T(8,128)S(1)} %convolution_bitcast_fusion.9), channel_id=1, replica_groups=mesh['grp'=4,'col'=8] {'grp','col'}, use_global_device_ids=true, to_apply=%region_18.21 | all-reduce | flops 768 | bytes 6144 | tf_op jit(solution)/shard_map/psum | solution.py:87
  541.8 41.4 %psum.77 = f32[16,16]{0,1:T(8,128)S(1)} all-reduce(f32[16,16]{0,1:T(8,128)S(1)} %fusion.184), channel_id=1, replica_groups=mesh['grp'=4,'col'=8] {'grp','col'}, use_global_device_ids=true, to_apply=%region_19.22 | all-reduce | flops 256 | bytes 2048 | tf_op jit(solution)/shard_map/psum | solution.py:90
  596.5 14.2 %all_gather.31 = f32[16,2048]{1,0:T(8,128)S(1)} all-gather(f32[16,256]{1,0:T(8,128)S(1)} %get-tuple-element.71), channel_id=1, replica_groups=mesh['grp'=4,'col'=8] {'col'}, dimensions={1}, use_global_device_ids=true | all-gather | bytes 147456 | tf_op jit(solution)/shard_map/all_gather | solution.py:77
  631.6 20.4 %reduce-scatter.29.cloned.1.call-done = f32[16,256]{1,0:T(8,128)} async-done(((f32[16,1024]{1,0:T(8,128)}), f32[16,256]{1,0:T(8,128)}) %reduce-scatter.29.cloned.1.call-update) | async-done | bytes 16400 | tf_op jit(solution)/shard_map/reduce_scatter | solution.py:63
  652.0 33.3 %reduce-scatter.27.cloned.1.call-done = f32[16,256]{1,0:T(8,128)} async-done(((f32[16,2048]{1,0:T(8,128)}), f32[16,256]{1,0:T(8,128)}) %reduce-scatter.27.cloned.1.call-update) | async-done | bytes 16400 | tf_op jit(solution)/shard_map/reduce_scatter | solution.py:62
  686.2 37.9 %psum.78 = f32[4,16,16]{1,2,0:T(8,128)S(1)} all-reduce(f32[4,16,16]{1,2,0:T(8,128)S(1)} %convolution_bitcast_fusion.8), channel_id=1, replica_groups=mesh['grp'=4,'col'=8] {'grp','col'}, use_global_device_ids=true, to_apply=%region_22.25 | all-reduce | flops 1024 | bytes 8192 | tf_op jit(solution)/shard_map/psum | solution.py:87
  724.5 41.4 %psum.79 = f32[16,16]{0,1:T(8,128)S(1)} all-reduce(f32[16,16]{0,1:T(8,128)S(1)} %fusion.185), channel_id=1, replica_groups=mesh['grp'=4,'col'=8] {'grp','col'}, use_global_device_ids=true, to_apply=%region_23.26 | all-reduce | flops 256 | bytes 2048 | tf_op jit(solution)/shard_map/psum | solution.py:90
  (159 shorter events, 138.9 us)
Async XLA Ops:
  7.2 9.0 %copy-start = (f32[16,256]{1,0:T(8,128)S(1)}, f32[16,256]{1,0:T(8,128)}, u32[]{:S(2)}) copy-start(f32[16,256]{1,0:T(8,128)} %param.16) | copy-start | bytes 49156
  7.2 7.3 copy-start.3
  7.2 82.3 %reduce-scatter.33.cloned.1.call-start = ((), (), s32[]{:S(2)}) async-start(), calls=%async_computation.19 | async-start | bytes 655360
  14.4 76.1 %reduce-scatter.31.cloned.1.call-start = ((), (), s32[]{:S(2)}) async-start(), calls=%async_computation.18 | async-start | bytes 1179648
  16.1 87.0 %reduce-scatter.17.cloned.1.call-start = ((), (), s32[]{:S(2)}) async-start(), calls=%async_computation.11 | async-start | bytes 81920 | tf_op jit(solution)/shard_map/reduce_scatter | solution.py:63
  70.0 66.4 %reduce-scatter.15.cloned.1.call-start = ((), (), s32[]{:S(2)}) async-start(), calls=%async_computation.10 | async-start | bytes 147456 | tf_op jit(solution)/shard_map/reduce_scatter | solution.py:62
  88.7 197.8 %reduce-scatter.21.cloned.1.call-start = ((), (), s32[]{:S(2)}) async-start(), calls=%async_computation.13 | async-start | bytes 81920 | tf_op jit(solution)/shard_map/reduce_scatter | solution.py:63
  264.1 55.8 %reduce-scatter.19.cloned.1.call-start = ((), (), s32[]{:S(2)}) async-start(), calls=%async_computation.12 | async-start | bytes 147456 | tf_op jit(solution)/shard_map/reduce_scatter | solution.py:62
  265.5 203.6 %reduce-scatter.25.cloned.1.call-start = ((), (), s32[]{:S(2)}) async-start(), calls=%async_computation.15 | async-start | bytes 81920 | tf_op jit(solution)/shard_map/reduce_scatter | solution.py:63
  446.6 55.9 %reduce-scatter.23.cloned.1.call-start = ((), (), s32[]{:S(2)}) async-start(), calls=%async_computation.14 | async-start | bytes 147456 | tf_op jit(solution)/shard_map/reduce_scatter | solution.py:62
  448.1 203.9 %reduce-scatter.29.cloned.1.call-start = ((), (), s32[]{:S(2)}) async-start(), calls=%async_computation.17 | async-start | bytes 81920 | tf_op jit(solution)/shard_map/reduce_scatter | solution.py:63
  629.5 55.8 %reduce-scatter.27.cloned.1.call-start = ((), (), s32[]{:S(2)}) async-start(), calls=%async_computation.16 | async-start | bytes 147456 | tf_op jit(solution)/shard_map/reduce_scatter | solution.py:62
  771.4 0.6 copy-start.2
  772.0 0.6 copy-start.1
Sparse Core Ops, SparseCore 0:
  14.5 27.8 reduce-scatter.32
  44.6 32.7 reduce-scatter.30
  80.8 22.2 reduce-scatter.16
  105.7 30.5 reduce-scatter.14
  264.2 22.3 reduce-scatter.20
  289.3 30.5 reduce-scatter.18
  446.7 22.3 reduce-scatter.24
  471.9 30.5 reduce-scatter.22
  629.6 22.3 reduce-scatter.28
  654.7 30.5 reduce-scatter.26
